TPU v7x, 128 devices: a whole 4x4x4 slice. The times are simulated.
128 devices in a mesh: body: 2 (over core), sub: 64 (over x, y, z).
Axes of the slice: x: 4, y: 4, z: 4, core: 2. Of those that a mesh axis runs over, the one named last changes fastest.
Arguments:
- rhs: float32 [8, 4096, 256], P(None, 'sub'), may hold values from -50 to 50
- compliance: float32 [4096, 256], P('sub'), may hold values from 0.5 to 2
- plate_owner: int32 [4096, 1], P('sub'), may hold values from 0 to 63; in each aligned block of 64 rows (0 to 63, 64 to 127, ...) at most 2 rows name the same one
- found_owner: int32 [4096, 1], P('sub'), may hold values from 0 to 63; in each aligned block of 64 rows (0 to 63, 64 to 127, ...) at most 2 rows name the same one
- slot_pairs: int32 [4096, 2], P('sub'), may hold values from 0 to 7
- active: int32 [4096], P('sub'), may hold values 0 or 1
- inverse: bfloat16 [2, 64, 2048, 2048], P('body', 'sub'), may hold values from -0.06 to 4, as said below
Outputs:
- multipliers: float32 [8, 4096, 256], P(None, 'sub')
Inputs may be any that keep to these rules, and one draw needn't show every extreme that they name: `plate_owner`: at most 2 patches among the list of one index of sub name the same plate substructure; some list names one exactly 2 times. `found_owner`: at most 2 patches among the list of one index of sub name the same foundation substructure; some list names one exactly 2 times. Each block inverse[b, t] is symmetric positive definite.
All inputs are finite; a program needn't handle non-finite values. No bound on the sum of `active` on one device may be relied on, other than what follows from the above.
Results may differ from a plain program's by a relative error of at most 0.0055.
Values sent between devices are 32-bit elements; how exact they have to be, the bound alone decides.
A program may use at most 64 MiB of HBM per device.

v0:
```python
import jax
import jax.numpy as jnp
from jax import lax
from jax.sharding import PartitionSpec as P

ITERS = 4


def products(left, right):
    return jnp.sum(left * right, axis=(1, 2))


def squares(residual):
    return lax.psum(products(residual, residual), "sub")


def on_device(rhs, compliance, plate_owner, found_owner, slot_pairs, active, inverse):
    nsub = lax.axis_size("sub")
    side = lax.axis_index("body")
    ncase, npatch, block_width = rhs.shape
    local_inverse_block = inverse[0, 0]
    number_of_slots = local_inverse_block.shape[0] // block_width
    room = max(2, 2 * npatch // nsub)
    nrow = nsub * room
    owner = jnp.where(side == 0, plate_owner[:, 0], found_owner[:, 0])
    slot = jnp.where(side == 0, slot_pairs[:, 0], slot_pairs[:, 1])
    patch_index = jnp.arange(npatch, dtype=jnp.int32)
    earlier = patch_index[None, :] < patch_index[:, None]
    same_owner = owner[None, :] == owner[:, None]
    rank = jnp.sum(jnp.where(earlier & same_owner, 1, 0), axis=1).astype(jnp.int32)
    dest_row = owner * room + rank
    placed = dest_row[None, :] == jnp.arange(nrow, dtype=jnp.int32)[:, None]
    source = jnp.sum(jnp.where(placed, patch_index[None, :], 0), axis=1)
    filled = jnp.any(placed, axis=1)
    sent_slot = jnp.where(filled, jnp.take(slot, source), -1)
    received_slot = lax.all_to_all(sent_slot, "sub", split_axis=0, concat_axis=0, tiled=True)
    slot_lookup_table = (
        received_slot[None, :] == jnp.arange(number_of_slots, dtype=jnp.int32)[:, None]
    ).astype(jnp.float32)
    send_valid = filled.astype(jnp.float32)[None, :, None]
    keep = active.astype(jnp.float32)[None, :, None]
    residual = keep * rhs
    solution = jnp.zeros_like(rhs)
    direction = residual
    norm_now = squares(residual)
    for step in range(ITERS):
        outgoing = jnp.take(direction, source, axis=1) * send_valid
        column_entries = lax.all_to_all(outgoing, "sub", split_axis=1, concat_axis=1, tiled=True)
        load_vectors = jnp.einsum(
            "sb,rbk->rsk", slot_lookup_table, column_entries, precision=lax.Precision.HIGHEST
        )
        load_vectors = load_vectors.reshape(
            column_entries.shape[0], number_of_slots * block_width
        ).astype(jnp.bfloat16)
        response = jnp.dot(load_vectors, local_inverse_block, preferred_element_type=jnp.float32)
        plate_piece = lax.all_gather(response[None], "sub", axis=0, tiled=True)
        start = jnp.int32(0)
        slot_count = plate_piece.shape[0]
        local = jnp.clip(owner, 0, slot_count - 1)
        block_list = plate_piece.reshape(
            slot_count, plate_piece.shape[1], number_of_slots, block_width
        )
        chosen = block_list[local, :, slot, :]
        inside = (owner >= start) & (owner < start + slot_count)
        own_part = jnp.transpose(jnp.where(inside[:, None, None], chosen, 0.0), (1, 0, 2))
        total = lax.psum(own_part, "body")
        image = keep * (total + compliance[None] * direction)
        alpha = norm_now / lax.psum(products(direction, image), "sub")
        solution = solution + alpha[:, None, None] * direction
        residual = residual - alpha[:, None, None] * image
        norm_next = squares(residual)
        direction = residual + (norm_next / norm_now)[:, None, None] * direction
        norm_now = norm_next
    return solution


def solution(mesh):
    in_specs = (
        P(None, "sub", None),
        P("sub", None),
        P("sub", None),
        P("sub", None),
        P("sub", None),
        P("sub"),
        P("body", "sub", None, None),
    )
    out_specs = P(None, "sub", None)
    return jax.shard_map(
        on_device, mesh=mesh, in_specs=in_specs, out_specs=out_specs, check_vma=False
    )
```

profile of v0, /device:TPU:1, one launch (start us, length us, event | category | flops | bytes accessed | tf_op | source)
XLA Modules:
  0.0 1729.7 jit_solution(2245857336711810583)
XLA Ops:
  6.5 0.7 compare_and_fusion.1
  7.7 0.8 fusion.33
  8.7 1.2 gather_fusion
  10.0 0.6 select_select_fusion
  10.7 12.0 all-to-all-start.1
  22.7 0.7 convert_element_type.47
  23.3 1.4 copy_multiply_fusion
  24.7 0.8 gather_fusion.5
  25.5 1.3 bitcast_multiply_fusion.3
  26.8 4.2 all-to-all-done.1
  31.0 5.6 all-to-all-start
  36.6 0.5 broadcast.252
  37.2 0.7 reduce.3
  38.0 14.7 all-to-all-done
  52.7 0.7 fusion.8
  53.5 5.3 fusion.6
  58.8 66.7 %all-gather.9.cloned.1.call-done = f32[512,2048]{1,0:T(8,128)} async-done(((f32[8,2048]{1,0:T(8,128)}), f32[512,2048]{1,0:T(8,128)}) %all-gather.9.cloned.1.call-update) | async-done | bytes 4194320 | tf_op jit(solution)/shard_map/all_gather | solution.py:56
  125.6 2.9 gather_fusion.1
  128.5 0.9 select_bitcast_fusion.3
  129.5 23.2 %all-reduce.6.cloned.1.call-done = f32[8,64,256]{2,0,1:T(8,128)} async-done(((f32[8,64,256]{2,0,1:T(8,128)}), f32[8,64,256]{2,0,1:T(8,128)}) %all-reduce.6.cloned.1.call-update) | async-done | bytes 524304 | tf_op jit(solution)/shard_map/psum | solution.py:66
  152.7 1.6 multiply_reduce_fusion.6
  154.3 151.0 %all-reduce = (f32[8]{0:T(128)S(1)}, f32[8]{0:T(128)S(1)}) all-reduce(f32[8]{0:T(128)S(1)} %get-tuple-element.7, f32[8]{0:T(128)S(1)} %get-tuple-element.6), channel_id=1, replica_groups=mesh['body'=2,'sub'=64] {'sub'}, use_global_device_ids=true, to_apply=%region_1.2 | all-reduce | flops 16 | bytes 128 | tf_op jit(solution)/shard_map/psum | solution.py:14
  305.3 1.6 multiply_reduce_fusion.5
  306.9 144.3 %psum.87 = f32[8]{0:T(128)S(1)} all-reduce(f32[8]{0:T(128)S(1)} %multiply_reduce_fusion.5), channel_id=1, replica_groups=mesh['body'=2,'sub'=64] {'sub'}, use_global_device_ids=true, to_apply=%region_9.11 | all-reduce | flops 8 | bytes 64 | tf_op jit(solution)/shard_map/psum | solution.py:14
  451.2 1.4 multiply_add_fusion.3
  452.6 0.8 gather_fusion.6
  453.4 0.3 bitcast_multiply_fusion.2
  453.7 17.0 all_to_all.26
  470.7 0.7 fusion.9
  471.5 5.3 fusion.4
  476.8 120.9 %all-gather.11.cloned.1.call-done = f32[512,2048]{1,0:T(8,128)} async-done(((f32[8,2048]{1,0:T(8,128)}), f32[512,2048]{1,0:T(8,128)}) %all-gather.11.cloned.1.call-update) | async-done | bytes 4194320 | tf_op jit(solution)/shard_map/all_gather | solution.py:56
  597.7 2.9 gather_fusion.2
  600.6 0.9 select_bitcast_fusion.2
  601.6 23.2 %all-reduce.8.cloned.1.call-done = f32[8,64,256]{2,0,1:T(8,128)} async-done(((f32[8,64,256]{2,0,1:T(8,128)}), f32[8,64,256]{2,0,1:T(8,128)}) %all-reduce.8.cloned.1.call-update) | async-done | bytes 524304 | tf_op jit(solution)/shard_map/psum | solution.py:66
  624.8 1.4 multiply_reduce_fusion.4
  626.1 151.1 %psum.89 = f32[8]{0:T(128)S(1)} all-reduce(f32[8]{0:T(128)S(1)} %multiply_reduce_fusion.4), channel_id=1, replica_groups=mesh['body'=2,'sub'=64] {'sub'}, use_global_device_ids=true, to_apply=%region_12.14 | all-reduce | flops 8 | bytes 64 | tf_op jit(solution)/shard_map/psum | solution.py:68
  777.3 1.7 multiply_reduce_fusion.3
  778.9 144.3 %psum.90 = f32[8]{0:T(128)S(1)} all-reduce(f32[8]{0:T(128)S(1)} %get-tuple-element.10), channel_id=1, replica_groups=mesh['body'=2,'sub'=64] {'sub'}, use_global_device_ids=true, to_apply=%region_14.16 | all-reduce | flops 8 | bytes 64 | tf_op jit(solution)/shard_map/psum | solution.py:14
  923.4 0.8 gather_fusion.7
  924.5 17.0 all_to_all.27
  941.5 0.7 fusion.10
  942.2 5.2 fusion.2
  947.5 120.5 %all-gather.13.cloned.1.call-done = f32[512,2048]{1,0:T(8,128)} async-done(((f32[8,2048]{1,0:T(8,128)}), f32[512,2048]{1,0:T(8,128)}) %all-gather.13.cloned.1.call-update) | async-done | bytes 4194320 | tf_op jit(solution)/shard_map/all_gather | solution.py:56
  1068.0 2.9 gather_fusion.3
  1070.9 0.9 select_bitcast_fusion.1
  1071.9 23.2 %all-reduce.10.cloned.1.call-done = f32[8,64,256]{2,0,1:T(8,128)} async-done(((f32[8,64,256]{2,0,1:T(8,128)}), f32[8,64,256]{2,0,1:T(8,128)}) %all-reduce.10.cloned.1.call-update) | async-done | bytes 524304 | tf_op jit(solution)/shard_map/psum | solution.py:66
  1095.1 1.4 multiply_reduce_fusion.2
  1096.4 151.0 %psum.92 = f32[8]{0:T(128)S(1)} all-reduce(f32[8]{0:T(128)S(1)} %multiply_reduce_fusion.2), channel_id=1, replica_groups=mesh['body'=2,'sub'=64] {'sub'}, use_global_device_ids=true, to_apply=%region_17.19 | all-reduce | flops 8 | bytes 64 | tf_op jit(solution)/shard_map/psum | solution.py:68
  1247.4 1.4 multiply_reduce_fusion.1
  1248.8 144.3 %psum.93 = f32[8]{0:T(128)S(1)} all-reduce(f32[8]{0:T(128)S(1)} %multiply_reduce_fusion.1), channel_id=1, replica_groups=mesh['body'=2,'sub'=64] {'sub'}, use_global_device_ids=true, to_apply=%region_19.21 | all-reduce | flops 8 | bytes 64 | tf_op jit(solution)/shard_map/psum | solution.py:14
  1393.1 1.2 multiply_add_fusion.1
  1394.3 1.7 gather_fusion.8
  1396.1 1.6 bitcast_multiply_fusion
  1397.6 17.0 all_to_all.28
  1414.6 0.7 fusion.11
  1415.4 5.2 fusion
  1420.6 121.5 %all-gather.15.cloned.1.call-done = f32[512,2048]{1,0:T(8,128)} async-done(((f32[8,2048]{1,0:T(8,128)}), f32[512,2048]{1,0:T(8,128)}) %all-gather.15.cloned.1.call-update) | async-done | bytes 4194320 | tf_op jit(solution)/shard_map/all_gather | solution.py:56
  1542.2 2.9 gather_fusion.4
  1545.1 0.9 select_bitcast_fusion
  1546.0 23.2 %all-reduce.12.cloned.1.call-done = f32[8,64,256]{2,0,1:T(8,128)} async-done(((f32[8,64,256]{2,0,1:T(8,128)}), f32[8,64,256]{2,0,1:T(8,128)}) %all-reduce.12.cloned.1.call-update) | async-done | bytes 524304 | tf_op jit(solution)/shard_map/psum | solution.py:66
  1569.2 1.4 multiply_reduce_fusion
  1570.6 151.0 %psum.95 = f32[8]{0:T(128)S(1)} all-reduce(f32[8]{0:T(128)S(1)} %multiply_reduce_fusion), channel_id=1, replica_groups=mesh['body'=2,'sub'=64] {'sub'}, use_global_device_ids=true, to_apply=%region_22.24 | all-reduce | flops 8 | bytes 64 | tf_op jit(solution)/shard_map/psum | solution.py:68
  1721.5 0.4 multiply_add_fusion
  1721.9 1.0 copy.27
  (49 shorter events, 2.0 us)
Async XLA Ops:
  10.7 20.3 %all-to-all-start.1 = ((s32[64,2,1]{1,2,0:T(1,128)}), s32[64,2,1]{1,2,0:T(1,128)S(1)}, u32[]{:S(2)}, u32[]{:S(2)}) async-start(s32[64,2,1]{1,2,0:T(1,128)} %bitcast.5), calls=%async_computation.1 | async-start | bytes 65536 | tf_op jit(solution)/shard_map/all_to_all | solution.py:36
  31.0 21.8 %all-to-all-start = ((f32[8,128,256]{2,0,1:T(8,128)}), f32[8,128,256]{2,0,1:T(8,128)S(1)}, u32[]{:S(2)}, u32[]{:S(2)}) async-start(f32[8,128,256]{2,0,1:T(8,128)} %bitcast_multiply_fusion.3), calls=%async_computation | async-start | bytes 2097152 | tf_op jit(solution)/shard_map/all_to_all | solution.py:48
  36.6 89.0 %all-gather.9.cloned.1.call-start = ((), (), s32[]{:S(2)}) async-start(), calls=%async_computation.9 | async-start | bytes 4259840 | tf_op jit(solution)/shard_map/all_gather | solution.py:56
  53.5 99.2 %copy-start = (f32[8,64,256]{2,1,0:T(8,128)S(1)}, f32[8,64,256]{2,1,0:T(8,128)}, u32[]{:S(2)}) copy-start(f32[8,64,256]{2,1,0:T(8,128)} %param.9) | copy-start | bytes 1572868
  53.5 99.2 %copy-start.2 = (f32[64,256]{1,0:T(8,128)S(1)}, f32[64,256]{1,0:T(8,128)}, u32[]{:S(2)}) copy-start(f32[64,256]{1,0:T(8,128)} %param.10) | copy-start | bytes 196612
  58.8 93.9 %all-reduce.6.cloned.1.call-start = ((), (), s32[]{:S(2)}) async-start(), calls=%async_computation.5 | async-start | bytes 1048576 | tf_op jit(solution)/shard_map/psum | solution.py:66
  129.4 468.3 %all-gather.11.cloned.1.call-start = ((), (), s32[]{:S(2)}) async-start(), calls=%async_computation.10 | async-start | bytes 4259840 | tf_op jit(solution)/shard_map/all_gather | solution.py:56
  471.4 305.8 %copy-start.1 = (f32[8,64,256]{2,0,1:T(8,128)S(1)}, f32[8,64,256]{2,0,1:T(8,128)}, u32[]{:S(2)}) copy-start(f32[8,64,256]{2,0,1:T(8,128)} %all-reduce.6.cloned.1.call-done) | copy-start | bytes 1572868
  476.7 148.0 %all-reduce.8.cloned.1.call-start = ((), (), s32[]{:S(2)}) async-start(), calls=%async_computation.6 | async-start | bytes 1048576 | tf_op jit(solution)/shard_map/psum | solution.py:66
  601.6 466.4 %all-gather.13.cloned.1.call-start = ((), (), s32[]{:S(2)}) async-start(), calls=%async_computation.11 | async-start | bytes 4259840 | tf_op jit(solution)/shard_map/all_gather | solution.py:56
  947.4 147.6 %all-reduce.10.cloned.1.call-start = ((), (), s32[]{:S(2)}) async-start(), calls=%async_computation.7 | async-start | bytes 1048576 | tf_op jit(solution)/shard_map/psum | solution.py:66
  1071.8 470.3 %all-gather.15.cloned.1.call-start = ((), (), s32[]{:S(2)}) async-start(), calls=%async_computation.12 | async-start | bytes 4259840 | tf_op jit(solution)/shard_map/all_gather | solution.py:56
  1420.6 148.6 %all-reduce.12.cloned.1.call-start = ((), (), s32[]{:S(2)}) async-start(), calls=%async_computation.8 | async-start | bytes 1048576 | tf_op jit(solution)/shard_map/psum | solution.py:66
Sparse Core Ops, SparseCore 0:
  58.9 66.6 all-gather.8
  129.6 23.0 all-reduce.5
  476.9 120.8 all-gather.10
  601.7 23.0 all-reduce.7
  947.6 120.3 all-gather.12
  1072.0 23.0 all-reduce.9
  1420.7 121.4 all-gather.14
  1546.1 23.0 all-reduce.11
where the time goes:
time: 1760 us; the launch traced here: 1730 us
  blocking collectives  1090 us (62%)
  waiting for transfers between devices  541 us (31%)
  other arithmetic  26.1 us (1%)
  matrix products  23.8 us (1%)
  local copies, waits for them, and re-layouts  18.8 us (1%)
  starting transfers between devices  17.9 us (1%)
    psum x4, blocking collectives, squares(): return lax.psum(products(residual, residual), 'sub')  584 us
    psum x3, blocking collectives, on_device(): alpha = norm_now / lax.psum(products(direction, image), 'sub')  453 us
    all_gather x4, waiting for transfers between devices, on_device(): plate_piece = lax.all_gather(response[None], 'sub', axis=0, tiled=True)  430 us
    psum x4, waiting for transfers between devices, on_device(): total = lax.psum(own_part, 'body')  92.7 us
    all_to_all x3, blocking collectives, on_device(): lax.all_to_all(outgoing, 'sub', split_axis=1, concat_axis=1, tiled=True)  51 us
  transfers between devices with their start and end apart: 10, of which 10 were waited for; matrix products, arithmetic and copies ran while one was open for 0% of the time, Pallas kernels for 0%

commit v1 on v0

v1 whole, which is shorter than its diff:
```python
import functools
import jax
import jax.numpy as jnp
from jax import lax
from jax.experimental import pallas as pl
from jax.experimental.pallas import tpu as pltpu
from jax.sharding import PartitionSpec as P

ITERS = 4
GROUPS = 2
ROOM = 2
UNROLL = 8
MESH = pl.DeviceIdType.MESH
FWD_SEND, FWD_RECV, RET_SEND, RET_RECV, FS_SEND, FS_RECV, RS_SEND, RS_RECV = range(8)


def to_row(col):
    lane = lax.broadcasted_iota(jnp.int32, (8, 128), 1)
    sub = lax.broadcasted_iota(jnp.int32, (8, 128), 0)
    spread = jnp.where(lane == sub, jnp.broadcast_to(col, (8, 128)), 0.0)
    return jnp.sum(spread, axis=0, keepdims=True)


def to_col(row):
    lane = lax.broadcasted_iota(jnp.int32, (8, 128), 1)
    sub = lax.broadcasted_iota(jnp.int32, (8, 128), 0)
    spread = jnp.where(lane == sub, jnp.broadcast_to(row, (8, 128)), 0.0)
    return jnp.sum(spread, axis=1, keepdims=True)


def wait_bytes(ref, sem):
    pltpu.make_async_copy(ref, ref, sem).wait()


def kernel(
    nsub, npatch, nslot, width,
    src, own, rank, keep, rhs, comp, slots, inv_hbm, out,
    inv, res, dirn, sol, fsend, frecv, rsend, rrecv0, rrecv1, psend, precv,
    load, lhs, resp, slot_in, slot_sm, slot_vec, fsc, fsc_in, rsc, rsc_in,
    sems, psem_send, psem_recv, slot_send, slot_recv, misc,
):
    rrecv = (rrecv0, rrecv1)
    b = lax.axis_index("body")
    me = lax.axis_index("sub")
    tile = (8, width)
    top = lax.broadcasted_iota(jnp.int32, tile, 0) < 4
    half = npatch // 2

    def swap(v):
        return pltpu.roll(v, 4, 0)

    def peer(i):
        return lax.rem(me + i, nsub)

    def remote(src_ref, dst_ref, send, recv, p):
        return pltpu.make_async_remote_copy(
            src_ref=src_ref, dst_ref=dst_ref, send_sem=send, recv_sem=recv,
            device_id=(b, p), device_id_type=MESH,
        )

    barrier = pltpu.get_barrier_semaphore()

    def greet(i, c):
        pl.semaphore_signal(barrier, inc=1, device_id=(b, peer(i)), device_id_type=MESH)
        return c

    lax.fori_loop(1, nsub, greet, 0)
    pl.semaphore_signal(barrier, inc=1, device_id=(1 - b, me), device_id_type=MESH)

    inv_copy = pltpu.make_async_copy(inv_hbm, inv, misc)
    inv_copy.start()

    def start_residual(i, accs):
        accs = list(accs)
        for u in range(UNROLL):
            p = i * UNROLL + u
            v = rhs[p]
            w = swap(v)
            for g in range(GROUPS):
                t = jnp.where(top, v, w) if g == 0 else jnp.where(top, w, v)
                res[g, p] = t
                dirn[g, p] = jnp.zeros(tile, jnp.float32)
                sol[g, p] = jnp.zeros(tile, jnp.float32)
                accs[g] = accs[g] + t * t
        return tuple(accs)

    zero = jnp.zeros(tile, jnp.float32)
    accs = lax.fori_loop(0, npatch // UNROLL, start_residual, (zero,) * GROUPS)
    for g in range(GROUPS):
        for s in range(nslot):
            load[g, s] = zero

    pl.semaphore_wait(barrier, nsub)

    def send_slots(i, c):
        p = peer(i)
        remote(slots.at[p], slot_in.at[me], slot_send, slot_recv, p).start()
        return c

    lax.fori_loop(1, nsub, send_slots, 0)
    pltpu.make_async_copy(slots.at[me], slot_in.at[me], slot_recv).start()

    def pack_forward(g, t):
        a = res[g, src[t * ROOM]]
        z = res[g, src[t * ROOM + 1]]
        fsend[g, t] = jnp.where(top, a, z)

    def forward(g, acc):
        fsc[g] = to_row(jnp.sum(acc, axis=1, keepdims=True))

        def one(i, c):
            p = peer(i)
            pack_forward(g, p)
            remote(fsend.at[g, p], frecv.at[g, me], sems.at[FWD_SEND, g], sems.at[FWD_RECV, g], p).start()
            remote(fsc.at[g], fsc_in.at[g, me], sems.at[FS_SEND, g], sems.at[FS_RECV, g], p).start()
            return c

        lax.fori_loop(1, nsub, one, 0)
        pack_forward(g, me)
        pltpu.make_async_copy(fsend.at[g, me], frecv.at[g, me], sems.at[FWD_RECV, g]).start()
        pltpu.make_async_copy(fsc.at[g], fsc_in.at[g, me], sems.at[FS_RECV, g]).start()

    def receive_forward(g, rr):
        wait_bytes(frecv.at[g], sems.at[FWD_RECV, g])
        wait_bytes(fsc_in.at[g], sems.at[FS_RECV, g])
        wait_bytes(fsend.at[g, pl.ds(0, nsub - 1)], sems.at[FWD_SEND, g])
        wait_bytes(fsc_in.at[g, pl.ds(0, nsub - 1)], sems.at[FS_SEND, g])
        new = to_col(jnp.sum(fsc_in[g], axis=0))
        beta = jnp.broadcast_to(new / rr, tile)

        def gather(i, accs):
            accs = list(accs)
            for u in range(4):
                s = i * 4 + u
                v = frecv[g, s]
                which = slot_vec[s]
                for k in range(nslot):
                    accs[k] = accs[k] + jnp.where(which == k, v, 0.0)
            return tuple(accs)

        sums = lax.fori_loop(0, nsub // 4, gather, (zero,) * nslot)
        for k in range(nslot):
            v = sums[k]
            v = v + swap(v) + beta * load[g, k]
            load[g, k] = v
            high = v.astype(jnp.bfloat16).astype(jnp.float32)
            lhs[:, k * width:(k + 1) * width] = jnp.where(top, high, v - high).astype(jnp.bfloat16)

        def column(n, acc):
            cols = pl.ds(pl.multiple_of(n * width, width), width)
            o = jnp.dot(lhs[...], inv[:, cols], preferred_element_type=jnp.float32)
            o = o + swap(o)
            resp[n] = o
            return acc + load[g, n] * o

        acc = lax.fori_loop(0, nslot, column, zero)

        def turn(i, acc):
            rows = comp[pl.ds(pl.multiple_of(i * UNROLL, UNROLL), UNROLL), :]
            for u in range(UNROLL):
                p = i * UNROLL + u
                v = res[g, p] + beta * dirn[g, p]
                dirn[g, p] = v
                acc = acc + rows[u:u + 1, :] * (v * v)
            return acc

        acc2 = lax.fori_loop(0, npatch // UNROLL, turn, zero)
        acc = acc + jnp.where(b == 0, 1.0, 0.0) * acc2
        return new, acc

    def pack_return(g, s):
        a = resp[jnp.maximum(slot_sm[s, 0, 0], 0)]
        z = resp[jnp.maximum(slot_sm[s, 0, 1], 0)]
        rsend[g, s] = jnp.where(top, a, z)

    def send_back(g, acc, data):
        rsc[g] = to_row(jnp.sum(acc, axis=1, keepdims=True))

        def one(i, c):
            p = peer(i)
            if data:
                pack_return(g, p)
                remote(rsend.at[g, p], rrecv[g].at[me], sems.at[RET_SEND, g], sems.at[RET_RECV, g], p).start()
            remote(rsc.at[g], rsc_in.at[g, me], sems.at[RS_SEND, g], sems.at[RS_RECV, g], p).start()
            return c

        lax.fori_loop(1, nsub, one, 0)
        if data:
            pack_return(g, me)
            pltpu.make_async_copy(rsend.at[g, me], rrecv[g].at[me], sems.at[RET_RECV, g]).start()
        pltpu.make_async_copy(rsc.at[g], rsc_in.at[g, me], sems.at[RS_RECV, g]).start()

    def partner(g, par, first):
        span = pl.ds(first, half + 1 - first)
        return pltpu.make_async_remote_copy(
            src_ref=psend.at[g, span], dst_ref=precv.at[par, g, span],
            send_sem=psem_send.at[g], recv_sem=psem_recv.at[par, g],
            device_id=(1 - b, me), device_id_type=MESH,
        )

    def receive_scalars(g):
        wait_bytes(rsc_in.at[g], sems.at[RS_RECV, g])
        wait_bytes(rsc_in.at[g, pl.ds(0, nsub - 1)], sems.at[RS_SEND, g])
        part = jnp.broadcast_to(to_col(jnp.sum(rsc_in[g], axis=0)), tile)
        psend[g, half] = part
        return part

    def receive_return(g, par, rr):
        wait_bytes(rrecv[g], sems.at[RET_RECV, g])
        wait_bytes(rsend.at[g, pl.ds(0, nsub - 1)], sems.at[RET_SEND, g])
        part = receive_scalars(g)

        def pick(i, c):
            for u in range(4):
                p = i * 4 + u
                q = p + half
                a = rrecv[g][own[p]]
                z = rrecv[g][own[q]]
                a = jnp.where(rank[p] == 0, a, swap(a))
                z = jnp.where(rank[q] == 0, swap(z), z)
                psend[g, p] = jnp.where(top, a, z)
            return c

        lax.fori_loop(0, half // 4, pick, 0)
        copy = partner(g, par, 0)
        copy.start()
        copy.wait()
        alpha = rr / (part + precv[par, g, half])

        def update(i, acc):
            low = comp[pl.ds(pl.multiple_of(i * UNROLL, UNROLL), UNROLL), :]
            high = comp[pl.ds(pl.multiple_of(half + i * UNROLL, UNROLL), UNROLL), :]
            for u in range(UNROLL):
                p = i * UNROLL + u
                pair = psend[g, p] + precv[par, g, p]
                other = swap(pair)
                for rows, q, v in (
                    (low, p, jnp.where(top, pair, other)),
                    (high, p + half, jnp.where(top, other, pair)),
                ):
                    d = dirn[g, q]
                    image = keep[q] * v + rows[u:u + 1, :] * d
                    sol[g, q] = sol[g, q] + alpha * d
                    r = res[g, q] - alpha * image
                    res[g, q] = r
                    acc = acc + r * r
            return acc

        return lax.fori_loop(0, half // UNROLL, update, zero)

    for g in range(GROUPS):
        forward(g, accs[g])

    wait_bytes(slot_in, slot_recv)
    wait_bytes(slot_in.at[pl.ds(0, nsub - 1)], slot_send)
    slot_copy = pltpu.make_async_copy(slot_in, slot_sm, misc)
    inv_copy.wait()
    slot_copy.start()
    slot_copy.wait()

    def spread_slots(i, c):
        for u in range(4):
            s = i * 4 + u
            slot_vec[s] = jnp.where(top, slot_sm[s, 0, 0], slot_sm[s, 0, 1])
        return c

    lax.fori_loop(0, nsub // 4, spread_slots, 0)

    def iteration(k, rrs):
        rrs = list(rrs)
        for g in range(GROUPS):
            rrs[g], acc = receive_forward(g, rrs[g])
            send_back(g, acc, True)
        for g in range(GROUPS):
            acc = receive_return(g, lax.rem(k, 2), jnp.broadcast_to(rrs[g], tile))
            forward(g, acc)
        return tuple(rrs)

    one = jnp.ones((8, 1), jnp.float32)
    rrs = list(lax.fori_loop(0, ITERS - 1, iteration, (one,) * GROUPS))
    par = (ITERS - 1) % 2
    for g in range(GROUPS):
        rrs[g], acc = receive_forward(g, rrs[g])
        send_back(g, acc, False)
    alphas = []
    for g in range(GROUPS):
        part = receive_scalars(g)
        copy = partner(g, par, half)
        copy.start()
        copy.wait()
        alphas.append(jnp.broadcast_to(rrs[g], tile) / (part + precv[par, g, half]))

    def finish(i, c):
        for u in range(UNROLL):
            p = i * UNROLL + u
            a = sol[0, p] + alphas[0] * dirn[0, p]
            z = sol[1, p] + alphas[1] * dirn[1, p]
            out[p] = jnp.where(top, a, z)
        return c

    lax.fori_loop(0, npatch // UNROLL, finish, 0)


def on_device(nsub, rhs, compliance, plate_owner, found_owner, slot_pairs, active, inverse):
    side = lax.axis_index("body")
    ncase, npatch, width = rhs.shape
    iface = inverse.shape[-1]
    nslot = iface // width
    nrow = nsub * ROOM
    owner = jnp.where(side == 0, plate_owner[:, 0], found_owner[:, 0])
    slot = jnp.where(side == 0, slot_pairs[:, 0], slot_pairs[:, 1])
    patch = jnp.arange(npatch, dtype=jnp.int32)
    same = (patch[None, :] < patch[:, None]) & (owner[None, :] == owner[:, None])
    rank = jnp.sum(same.astype(jnp.int32), axis=1)
    placed = (owner * ROOM + rank)[None, :] == jnp.arange(nrow, dtype=jnp.int32)[:, None]
    source = jnp.sum(jnp.where(placed, patch[None, :], 0), axis=1)
    sent_slot = jnp.sum(jnp.where(placed, slot[None, :] + 1, 0), axis=1) - 1
    slots = jnp.pad(sent_slot.reshape(nsub, 1, ROOM), ((0, 0), (0, 0), (0, 128 - ROOM)))
    keep = active.astype(jnp.float32)
    masked = jnp.transpose(keep[None, :, None] * rhs, (1, 0, 2))
    comp = keep[:, None] * compliance

    f32, i32 = jnp.float32, jnp.int32
    vmem = pl.BlockSpec(memory_space=pltpu.VMEM)
    smem = pl.BlockSpec(memory_space=pltpu.SMEM)
    state = pltpu.VMEM((GROUPS, npatch, 8, width), f32)
    message = pltpu.VMEM((GROUPS, nsub, 8, width), f32)
    single = pltpu.VMEM((nsub, 8, width), f32)
    half = npatch // 2
    result = pl.pallas_call(
        functools.partial(kernel, nsub, npatch, nslot, width),
        out_shape=jax.ShapeDtypeStruct((npatch, ncase, width), f32),
        in_specs=[smem, smem, smem, smem, vmem, vmem, vmem, pl.BlockSpec(memory_space=pl.ANY)],
        out_specs=vmem,
        scratch_shapes=[
            pltpu.VMEM((iface, iface), jnp.bfloat16),
            state, state, state, message, message, message, single, single,
            pltpu.VMEM((GROUPS, half + 1, 8, width), f32),
            pltpu.VMEM((2, GROUPS, half + 1, 8, width), f32),
            pltpu.VMEM((GROUPS, nslot, 8, width), f32),
            pltpu.VMEM((8, iface), jnp.bfloat16),
            pltpu.VMEM((nslot, 8, width), f32),
            pltpu.VMEM((nsub, 1, 128), i32),
            pltpu.SMEM((nsub, 1, 128), i32),
            pltpu.VMEM((nsub, 8, width), i32),
            pltpu.VMEM((GROUPS, 1, 128), f32),
            pltpu.VMEM((GROUPS, nsub, 1, 128), f32),
            pltpu.VMEM((GROUPS, 1, 128), f32),
            pltpu.VMEM((GROUPS, nsub, 1, 128), f32),
            pltpu.SemaphoreType.DMA((8, GROUPS)),
            pltpu.SemaphoreType.DMA((GROUPS,)),
            pltpu.SemaphoreType.DMA((2, GROUPS)),
            pltpu.SemaphoreType.DMA,
            pltpu.SemaphoreType.DMA,
            pltpu.SemaphoreType.DMA,
        ],
        compiler_params=pltpu.CompilerParams(
            collective_id=0, has_side_effects=True, vmem_limit_bytes=48 * 2**20
        ),
    )(source, owner, rank, keep, masked, comp, slots, inverse[0, 0])
    return jnp.transpose(result, (1, 0, 2))


def solution(mesh):
    in_specs = (
        P(None, "sub", None),
        P("sub", None),
        P("sub", None),
        P("sub", None),
        P("sub", None),
        P("sub"),
        P("body", "sub", None, None),
    )
    return jax.shard_map(
        functools.partial(on_device, mesh.shape["sub"]),
        mesh=mesh, in_specs=in_specs, out_specs=P(None, "sub", None), check_vma=False,
    )
```

time: 1760 us -> 136 us (0.08); the launches traced: 1730 us -> 136 us
  blocking collectives: 1090 us -> 0 us
  waiting for transfers between devices: 541 us -> 0 us
  Pallas kernels: 0 us -> 131 us
  matrix products: 23.8 us -> 0 us
  other arithmetic: 26.1 us -> 3.98 us
  starting transfers between devices: 17.9 us -> 0 us
  local copies, waits for them, and re-layouts: 18.8 us -> 1.11 us
    psum x7 -> x0, blocking collectives: 1040 us -> none  [the longest x4 584 us: squares(): return lax.psum(products(residual, residual), 'sub')]
    all_gather x4 -> x0, waiting for transfers between devices: 430 us -> none  [on_device(): plate_piece = lax.all_gather(response[None], 'sub', axis=0, tiled=True)]
    pallas_call x0 -> x1, Pallas kernels: none -> 131 us  [on_device(): pl.pallas_call(functools.partial(kernel, nsub, npatch, nslot, width), out...]
    psum x4 -> x0, waiting for transfers between devices: 92.7 us -> none  [on_device(): total = lax.psum(own_part, 'body')]
    all_to_all x3 -> x0, blocking collectives: 51 us -> none  [on_device(): lax.all_to_all(outgoing, 'sub', split_axis=1, concat_axis=1, tiled=True)]
    dot_general x8 -> x0, matrix products: 23.8 us -> none  [the longest x4 21 us: on_device(): jnp.dot(load_vectors, local_inverse_block, preferred_element_type=jnp.flo...]
    all_to_all x2 -> x0, waiting for transfers between devices: 18.9 us -> none  [the longest x1 14.7 us: on_device(): lax.all_to_all(outgoing, 'sub', split_axis=1, concat_axis=1, tiled=True)]
  transfers between devices with their start and end apart: 10 -> 0, of which waited for: 10 -> 0; matrix products, arithmetic and copies ran while one was open for 0% -> 0% of each run, Pallas kernels for 0% -> 0%
where the time goes in v1:
time: 136 us
  Pallas kernels  131 us (96%)
  other arithmetic  3.98 us (3%)
    pallas_call x1, Pallas kernels, on_device(): pl.pallas_call(functools.partial(kernel, nsub, npatch, nslot, width), out...  131 us

profile of v1, /device:TPU:1, one launch (start us, length us, event | category | flops | bytes accessed | tf_op | source)
XLA Modules:
  0.0 136.1 jit_solution(11194994458477989787)
XLA Ops:
  0.0 0.7 convert_element_type.7.keep
  0.7 0.8 fusion.2
  1.4 0.2 convert_reduce_fusion.rank
  1.6 0.1 select_reduce_fusion
  1.7 0.1 sub.7
  1.9 0.9 broadcast_multiply_fusion.comp
  2.8 1.4 fusion.rhs
  4.2 130.9 %shard_map.73 = f32[64,8,256]{2,1,0:T(8,128)S(1)} custom-call(s32[128]{0:T(128)S(1)} %get-tuple-element.6.src, s32[64]{0:T(128)S(1)} %get-tuple-element.7.own, s32[64]{0:T(128)S(1)} %convert_reduce_fusion.rank, f32[64]{0:T(128)S(1)} %convert_element_type.7.keep, f32[64,8,256]{2,1,0:T(8,128)S(1)} %fusion.rhs, f32[64,256]{1,0:T(8,128)S(1)} %broadcast_multiply_fusion.comp, ...), custom_call_target="tpu_custom_call" | custom-call | tf_op jit(solution)/shard_map/pallas_call | solution.py:330
  135.1 1.0 copy.16
  (3 shorter events, 0.0 us)

commit v2 on v1

v2 whole, which is shorter than its diff:
```python
import functools
import jax
import jax.numpy as jnp
from jax import lax
from jax.experimental import pallas as pl
from jax.experimental.pallas import tpu as pltpu
from jax.sharding import PartitionSpec as P

ITERS = 4
GROUPS = 2
ROOM = 2
UNROLL = 8
ISSUE = 9
SPAN = 8
MESH = pl.DeviceIdType.MESH
FWD_SEND, FWD_RECV, RET_SEND, RET_RECV = range(4)
NEAR_SEND, NEAR_RECV, FAR_SEND, FAR_RECV, ALL_SEND, ALL_RECV = range(4, 10)


def to_row(col):
    lane = lax.broadcasted_iota(jnp.int32, (8, 128), 1)
    sub = lax.broadcasted_iota(jnp.int32, (8, 128), 0)
    spread = jnp.where(lane == sub, jnp.broadcast_to(col, (8, 128)), 0.0)
    return jnp.sum(spread, axis=0, keepdims=True)


def to_col(row):
    lane = lax.broadcasted_iota(jnp.int32, (8, 128), 1)
    sub = lax.broadcasted_iota(jnp.int32, (8, 128), 0)
    spread = jnp.where(lane == sub, jnp.broadcast_to(row, (8, 128)), 0.0)
    return jnp.sum(spread, axis=1, keepdims=True)


def wait_bytes(ref, sem):
    pltpu.make_async_copy(ref, ref, sem).wait()


def kernel(
    nsub, npatch, nslot, width,
    src, own, rank, keep, comp, slots, rhs_hbm, inv_hbm, out,
    inv, rhs, res, dirn, imag, sol, fsend, frecv, rsend, rrecv0, rrecv1, psend, precv,
    load, lhs, resp, slot_in, slot_sm, slot_vec, near, near_in, far, far_in, all_in,
    sems, psem_send, psem_recv, slot_send, slot_recv, rhs_sem, inv_sem, misc,
):
    rrecv = (rrecv0, rrecv1)
    b = lax.axis_index("body")
    me = lax.axis_index("sub")
    tile = (8, width)
    top = lax.broadcasted_iota(jnp.int32, tile, 0) < 4
    half = npatch // 2
    zero = jnp.zeros(tile, jnp.float32)

    def swap(v):
        return pltpu.roll(v, 4, 0)

    def peer(i):
        return lax.rem(me + i, nsub)

    def peers(body, unroll):
        def some(i, c):
            for u in range(unroll):
                body(peer(1 + i * unroll + u))
            return c

        whole = (nsub - 1) // unroll
        lax.fori_loop(0, whole, some, 0)
        for i in range(1 + whole * unroll, nsub):
            body(peer(i))

    def remote(src_ref, dst_ref, send, recv, p):
        return pltpu.make_async_remote_copy(
            src_ref=src_ref, dst_ref=dst_ref, send_sem=send, recv_sem=recv,
            device_id=(b, p), device_id_type=MESH,
        )

    rhs_copies = [
        pltpu.make_async_copy(rhs_hbm.at[c], rhs.at[:, c, :], rhs_sem.at[c]) for c in range(8)
    ]
    for copy in rhs_copies:
        copy.start()

    barrier = pltpu.get_barrier_semaphore()
    peers(
        lambda p: pl.semaphore_signal(barrier, inc=1, device_id=(b, p), device_id_type=MESH),
        ISSUE,
    )
    pl.semaphore_signal(barrier, inc=1, device_id=(1 - b, me), device_id_type=MESH)

    inv_copy = pltpu.make_async_copy(inv_hbm, inv, inv_sem)
    inv_copy.start()
    for copy in rhs_copies:
        copy.wait()

    def start_residual(i, accs):
        accs = list(accs)
        rows = comp[pl.ds(pl.multiple_of(i * UNROLL, UNROLL), UNROLL), :]
        for u in range(UNROLL):
            p = i * UNROLL + u
            v = keep[p] * rhs[p]
            w = swap(v)
            for g in range(GROUPS):
                t = jnp.where(top, v, w) if g == 0 else jnp.where(top, w, v)
                res[g, p] = t
                dirn[g, p] = zero
                imag[g, p] = zero
                sol[g, p] = zero
                square = t * t
                accs[g] = accs[g] + square
                accs[GROUPS + g] = accs[GROUPS + g] + rows[u:u + 1, :] * square
        return tuple(accs)

    accs = lax.fori_loop(0, npatch // UNROLL, start_residual, (zero,) * (2 * GROUPS))
    sums = [(accs[g], accs[GROUPS + g]) for g in range(GROUPS)]

    pl.semaphore_wait(barrier, nsub)

    def pack_forward(g, t):
        a = res[g, src[t * ROOM]]
        z = res[g, src[t * ROOM + 1]]
        fsend[g, t] = jnp.where(top, a, z)

    def forward(g):
        def one(p):
            pack_forward(g, p)
            remote(fsend.at[g, p], frecv.at[g, me], sems.at[FWD_SEND, g], sems.at[FWD_RECV, g], p).start()

        peers(one, ISSUE)
        pack_forward(g, me)
        pltpu.make_async_copy(fsend.at[g, me], frecv.at[g, me], sems.at[FWD_RECV, g]).start()

    def forward_sent(g):
        wait_bytes(fsend.at[g, pl.ds(0, nsub - 1)], sems.at[FWD_SEND, g])

    def return_sent(g):
        wait_bytes(rsend.at[g, pl.ds(0, nsub - 1)], sems.at[RET_SEND, g])

    def receive_forward(g):
        wait_bytes(frecv.at[g], sems.at[FWD_RECV, g])

        def gather(i, accs):
            accs = list(accs)
            for u in range(4):
                s = i * 4 + u
                v = frecv[g, s]
                which = slot_vec[s]
                for k in range(nslot):
                    accs[k] = accs[k] + jnp.where(which == k, v, 0.0)
            return tuple(accs)

        loads = lax.fori_loop(0, nsub // 4, gather, (zero,) * nslot)
        for k in range(nslot):
            v = loads[k] + swap(loads[k])
            load[k] = v
            high = v.astype(jnp.bfloat16).astype(jnp.float32)
            lhs[:, k * width:(k + 1) * width] = jnp.where(top, high, v - high).astype(jnp.bfloat16)

        def column(n, acc):
            cols = pl.ds(pl.multiple_of(n * width, width), width)
            o = jnp.dot(lhs[...], inv[:, cols], preferred_element_type=jnp.float32)
            o = o + swap(o)
            resp[n] = o
            return acc + load[n] * o

        return lax.fori_loop(0, nslot, column, zero)

    def pack_return(g, s):
        a = resp[jnp.maximum(slot_sm[s, 0, 0], 0)]
        z = resp[jnp.maximum(slot_sm[s, 0, 1], 0)]
        rsend[g, s] = jnp.where(top, a, z)

    def sums_row(loaded, squares):
        rr, rcr = squares
        image = loaded + jnp.where(b == 0, 1.0, 0.0) * rcr
        return to_row(jnp.sum(jnp.where(top, image, rr), axis=1, keepdims=True))

    block, place = me // SPAN, me % SPAN

    def send_near(g, row):
        near[g] = row
        for i in range(1, SPAN):
            p = block * SPAN + (place + i) % SPAN
            remote(near.at[g], near_in.at[g, place], sems.at[NEAR_SEND, g], sems.at[NEAR_RECV, g], p).start()
        pltpu.make_async_copy(near.at[g], near_in.at[g, place], sems.at[NEAR_RECV, g]).start()

    def send_far(g):
        wait_bytes(near_in.at[g], sems.at[NEAR_RECV, g])
        wait_bytes(near_in.at[g, pl.ds(0, SPAN - 1)], sems.at[NEAR_SEND, g])
        far[g] = jnp.sum(near_in[g], axis=0)
        for i in range(1, nsub // SPAN):
            p = (block + i) % (nsub // SPAN) * SPAN + place
            remote(far.at[g], far_in.at[g, block], sems.at[FAR_SEND, g], sems.at[FAR_RECV, g], p).start()
        pltpu.make_async_copy(far.at[g], far_in.at[g, block], sems.at[FAR_RECV, g]).start()

    def receive_far(g):
        wait_bytes(far_in.at[g], sems.at[FAR_RECV, g])
        wait_bytes(far_in.at[g, pl.ds(0, nsub // SPAN - 1)], sems.at[FAR_SEND, g])
        return jnp.sum(far_in[g], axis=0)

    def send_all(g, row):
        near[g] = row
        peers(
            lambda p: remote(near.at[g], all_in.at[g, me], sems.at[ALL_SEND, g], sems.at[ALL_RECV, g], p).start(),
            ISSUE,
        )
        pltpu.make_async_copy(near.at[g], all_in.at[g, me], sems.at[ALL_RECV, g]).start()

    def receive_all(g):
        wait_bytes(all_in.at[g], sems.at[ALL_RECV, g])
        wait_bytes(all_in.at[g, pl.ds(0, nsub - 1)], sems.at[ALL_SEND, g])
        return jnp.sum(all_in[g], axis=0)

    def send_back(g):
        def one(p):
            pack_return(g, p)
            remote(rsend.at[g, p], rrecv[g].at[me], sems.at[RET_SEND, g], sems.at[RET_RECV, g], p).start()

        peers(one, ISSUE)
        pack_return(g, me)
        pltpu.make_async_copy(rsend.at[g, me], rrecv[g].at[me], sems.at[RET_RECV, g]).start()

    def partner(g, par, part):
        first, size = ((0, 1 + half // 2), (1 + half // 2, half // 2), (0, 1))[part]
        return pltpu.make_async_remote_copy(
            src_ref=psend.at[g, pl.ds(first, size)], dst_ref=precv.at[par, g, pl.ds(first, size)],
            send_sem=psem_send.at[g, part % 2], recv_sem=psem_recv.at[par, g, part % 2],
            device_id=(1 - b, me), device_id_type=MESH,
        )

    def unfold(g, row):
        both = jnp.broadcast_to(to_col(row), tile)
        other = swap(both)
        image = jnp.where(top, both, other)
        psend[g, 0] = image
        return image, jnp.where(top, other, both)

    def steps(g, par, image, rr, rr_old, curve_old):
        beta = rr / rr_old
        return beta, image + precv[par, g, 0] - beta * beta * curve_old

    def receive_return(g, par, rr_old, curve_old):
        wait_bytes(rrecv[g], sems.at[RET_RECV, g])
        image, rr = unfold(g, receive_far(g))

        def pick(i, c):
            for u in range(4):
                p = i * 4 + u
                q = p + half
                a = rrecv[g][own[p]]
                z = rrecv[g][own[q]]
                a = jnp.where(rank[p] == 0, a, swap(a))
                z = jnp.where(rank[q] == 0, swap(z), z)
                psend[g, 1 + p] = jnp.where(top, a, z)
            return c

        lax.fori_loop(0, half // 8, pick, 0)
        first = partner(g, par, 0)
        first.start()
        lax.fori_loop(half // 8, half // 4, pick, 0)
        second = partner(g, par, 1)
        second.start()
        first.wait()
        beta, curve = steps(g, par, image, rr, rr_old, curve_old)
        alpha = rr / curve

        def update(i, accs):
            acc, acc2 = accs
            low = comp[pl.ds(pl.multiple_of(i * UNROLL, UNROLL), UNROLL), :]
            high = comp[pl.ds(pl.multiple_of(half + i * UNROLL, UNROLL), UNROLL), :]
            for u in range(UNROLL):
                p = i * UNROLL + u
                pair = psend[g, 1 + p] + precv[par, g, 1 + p]
                other = swap(pair)
                for rows, q, v in (
                    (low, p, jnp.where(top, pair, other)),
                    (high, p + half, jnp.where(top, other, pair)),
                ):
                    c = jnp.broadcast_to(rows[u:u + 1, :], tile)
                    r = res[g, q]
                    d = r + beta * dirn[g, q]
                    f = keep[q] * (v + c * r) + beta * imag[g, q]
                    dirn[g, q] = d
                    imag[g, q] = f
                    sol[g, q] = sol[g, q] + alpha * d
                    r = r - alpha * f
                    res[g, q] = r
                    square = r * r
                    acc = acc + square
                    acc2 = acc2 + c * square
            return acc, acc2

        squares = lax.fori_loop(0, half // UNROLL // 2, update, (zero, zero))
        second.wait()
        squares = lax.fori_loop(half // UNROLL // 2, half // UNROLL, update, squares)
        return squares, rr, curve

    forward(0)
    peers(lambda p: remote(slots.at[p], slot_in.at[me], slot_send, slot_recv, p).start(), ISSUE)
    pltpu.make_async_copy(slots.at[me], slot_in.at[me], slot_recv).start()
    forward_sent(0)
    forward(1)

    wait_bytes(slot_in, slot_recv)
    wait_bytes(slot_in.at[pl.ds(0, nsub - 1)], slot_send)
    slot_copy = pltpu.make_async_copy(slot_in, slot_sm, misc)
    slot_copy.start()
    inv_copy.wait()
    slot_copy.wait()

    def spread_slots(i, c):
        for u in range(4):
            s = i * 4 + u
            slot_vec[s] = jnp.where(top, slot_sm[s, 0, 0], slot_sm[s, 0, 1])
        return c

    lax.fori_loop(0, nsub // 4, spread_slots, 0)

    def iteration(k, carry):
        carry = list(carry)
        for g in range(GROUPS):
            row = sums_row(receive_forward(g), carry[g][0])
            if g > 0:
                send_far(g - 1)
            send_near(g, row)
            (forward_sent if g == 0 else return_sent)(1 - g)
            send_back(g)
        for g in range(GROUPS):
            carry[g] = receive_return(g, lax.rem(k, 2), *carry[g][1:])
            if g == 0:
                send_far(GROUPS - 1)
            (return_sent if g == 0 else forward_sent)(1 - g)
            forward(g)
        return tuple(carry)

    one = jnp.ones(tile, jnp.float32)
    carry = lax.fori_loop(0, ITERS - 1, iteration, tuple((sums[g], one, zero) for g in range(GROUPS)))
    par = (ITERS - 1) % 2
    for g in range(GROUPS):
        send_all(g, sums_row(receive_forward(g), carry[g][0]))
        if g == 0:
            forward_sent(1)
    last = []
    for g in range(GROUPS):
        image, rr = unfold(g, receive_all(g))
        copy = partner(g, par, 2)
        copy.start()
        copy.wait()
        beta, curve = steps(g, par, image, rr, carry[g][1], carry[g][2])
        last.append((rr / curve, beta))

    def finish(i, c):
        for u in range(UNROLL):
            p = i * UNROLL + u
            a, z = (
                sol[g, p] + last[g][0] * (res[g, p] + last[g][1] * dirn[g, p]) for g in range(GROUPS)
            )
            out[p] = jnp.where(top, a, z)
        return c

    lax.fori_loop(0, npatch // UNROLL, finish, 0)


def on_device(nsub, rhs, compliance, plate_owner, found_owner, slot_pairs, active, inverse):
    side = lax.axis_index("body")
    ncase, npatch, width = rhs.shape
    iface = inverse.shape[-1]
    nslot = iface // width
    nrow = nsub * ROOM
    owner = jnp.where(side == 0, plate_owner[:, 0], found_owner[:, 0])
    slot = jnp.where(side == 0, slot_pairs[:, 0], slot_pairs[:, 1])
    patch = jnp.arange(npatch, dtype=jnp.int32)
    same = (patch[None, :] < patch[:, None]) & (owner[None, :] == owner[:, None])
    rank = jnp.sum(same.astype(jnp.int32), axis=1)
    placed = (owner * ROOM + rank)[None, :] == jnp.arange(nrow, dtype=jnp.int32)[:, None]
    source = jnp.sum(jnp.where(placed, patch[None, :], 0), axis=1)
    sent_slot = jnp.sum(jnp.where(placed, slot[None, :] + 1, 0), axis=1) - 1
    slots = jnp.pad(sent_slot.reshape(nsub, 1, ROOM), ((0, 0), (0, 0), (0, 128 - ROOM)))
    keep = active.astype(jnp.float32)

    f32, i32 = jnp.float32, jnp.int32
    vmem = pl.BlockSpec(memory_space=pltpu.VMEM)
    smem = pl.BlockSpec(memory_space=pltpu.SMEM)
    hbm = pl.BlockSpec(memory_space=pl.ANY)
    state = pltpu.VMEM((GROUPS, npatch, 8, width), f32)
    message = pltpu.VMEM((GROUPS, nsub, 8, width), f32)
    single = pltpu.VMEM((nsub, 8, width), f32)
    half = npatch // 2
    result = pl.pallas_call(
        functools.partial(kernel, nsub, npatch, nslot, width),
        out_shape=jax.ShapeDtypeStruct((npatch, ncase, width), f32),
        in_specs=[smem, smem, smem, smem, vmem, vmem, hbm, hbm],
        out_specs=vmem,
        scratch_shapes=[
            pltpu.VMEM((iface, iface), jnp.bfloat16),
            single, state, state, state, state, message, message, message, single, single,
            pltpu.VMEM((GROUPS, half + 1, 8, width), f32),
            pltpu.VMEM((2, GROUPS, half + 1, 8, width), f32),
            pltpu.VMEM((nslot, 8, width), f32),
            pltpu.VMEM((8, iface), jnp.bfloat16),
            pltpu.VMEM((nslot, 8, width), f32),
            pltpu.VMEM((nsub, 1, 128), i32),
            pltpu.SMEM((nsub, 1, 128), i32),
            pltpu.VMEM((nsub, 8, width), i32),
            pltpu.VMEM((GROUPS, 1, 128), f32),
            pltpu.VMEM((GROUPS, SPAN, 1, 128), f32),
            pltpu.VMEM((GROUPS, 1, 128), f32),
            pltpu.VMEM((GROUPS, nsub // SPAN, 1, 128), f32),
            pltpu.VMEM((GROUPS, nsub, 1, 128), f32),
            pltpu.SemaphoreType.DMA((10, GROUPS)),
            pltpu.SemaphoreType.DMA((GROUPS, 2)),
            pltpu.SemaphoreType.DMA((2, GROUPS, 2)),
            pltpu.SemaphoreType.DMA,
            pltpu.SemaphoreType.DMA,
            pltpu.SemaphoreType.DMA((8,)),
            pltpu.SemaphoreType.DMA,
            pltpu.SemaphoreType.DMA,
        ],
        compiler_params=pltpu.CompilerParams(
            collective_id=0, has_side_effects=True, vmem_limit_bytes=48 * 2**20
        ),
    )(source, owner, rank, keep, compliance, slots, rhs, inverse[0, 0])
    return jnp.transpose(result, (1, 0, 2))


def solution(mesh):
    in_specs = (
        P(None, "sub", None),
        P("sub", None),
        P("sub", None),
        P("sub", None),
        P("sub", None),
        P("sub"),
        P("body", "sub", None, None),
    )
    return jax.shard_map(
        functools.partial(on_device, mesh.shape["sub"]),
        mesh=mesh, in_specs=in_specs, out_specs=P(None, "sub", None), check_vma=False,
    )
```

time: 136 us -> 130 us (0.956)
  Pallas kernels: 131 us -> 125 us
  other arithmetic: 3.98 us -> 1.71 us
  local copies, waits for them, and re-layouts: 1.11 us -> 2.99 us
    pallas_call x1, Pallas kernels: 131 us -> 125 us  [on_device(): pl.pallas_call(functools.partial(kernel, nsub, npatch, nslot, width), out...]
    unnamed x0 -> x4, local copies, waits for them, and re-layouts: none -> 1.88 us
where the time goes in v2:
time: 130 us
  Pallas kernels  125 us (96%)
  local copies, waits for them, and re-layouts  2.99 us (2%)
  other arithmetic  1.71 us (1%)
    pallas_call x1, Pallas kernels, on_device(): pl.pallas_call(functools.partial(kernel, nsub, npatch, nslot, width), out...  125 us

profile of v2, /device:TPU:1, one launch (start us, length us, event | category | flops | bytes accessed | tf_op | source)
XLA Modules:
  0.0 129.9 jit_solution(6464838791100220794)
XLA Ops:
  0.0 0.7 convert_element_type.7.keep
  0.7 0.8 fusion.1
  1.4 0.2 convert_reduce_fusion.rank
  1.6 0.1 select_reduce_fusion
  1.7 0.1 sub.7
  1.9 0.0 copy-start
  1.9 1.0 copy-done
  2.9 0.0 copy-start.1
  2.9 0.8 copy-done.1
  3.8 125.2 %shard_map.73 = f32[64,8,256]{2,1,0:T(8,128)S(1)} custom-call(s32[128]{0:T(128)S(1)} %get-tuple-element.6.src, s32[64]{0:T(128)S(1)} %get-tuple-element.7.own, s32[64]{0:T(128)S(1)} %convert_reduce_fusion.rank, f32[64]{0:T(128)S(1)} %convert_element_type.7.keep, f32[64,256]{1,0:T(8,128)S(1)} %copy-done.1, s32[64,1,128]{2,1,0:T(1,128)S(1)} %pad.4.slots, ...), custom_call_target="tpu_custom_call" | custom-call | tf_op jit(solution)/shard_map/pallas_call | solution.py:387
  129.0 1.0 copy.13
  (3 shorter events, 0.0 us)
Async XLA Ops:
  1.9 1.0 copy-start
  2.9 0.8 copy-start.1

commit v3 on v2

--- a/solution.py
+++ b/solution.py
@@ -10,8 +10,9 @@
 GROUPS = 2
 ROOM = 2
 UNROLL = 8
-ISSUE = 9
+ISSUE = 3
 SPAN = 8
+CUT = 60
 MESH = pl.DeviceIdType.MESH
 FWD_SEND, FWD_RECV, RET_SEND, RET_RECV = range(4)
 NEAR_SEND, NEAR_RECV, FAR_SEND, FAR_RECV, ALL_SEND, ALL_RECV = range(4, 10)
@@ -56,15 +57,17 @@
     def peer(i):
         return lax.rem(me + i, nsub)
 
-    def peers(body, unroll):
+    def peers(body, unroll, first=1, stop=None):
+        stop = nsub if stop is None else stop
+
         def some(i, c):
             for u in range(unroll):
-                body(peer(1 + i * unroll + u))
+                body(peer(first + i * unroll + u))
             return c
 
-        whole = (nsub - 1) // unroll
+        whole = (stop - first) // unroll
         lax.fori_loop(0, whole, some, 0)
-        for i in range(1 + whole * unroll, nsub):
+        for i in range(first + whole * unroll, stop):
             body(peer(i))
 
     def remote(src_ref, dst_ref, send, recv, p):
@@ -119,12 +122,14 @@
         z = res[g, src[t * ROOM + 1]]
         fsend[g, t] = jnp.where(top, a, z)
 
-    def forward(g):
+    def forward(g, first=1, stop=nsub):
         def one(p):
             pack_forward(g, p)
             remote(fsend.at[g, p], frecv.at[g, me], sems.at[FWD_SEND, g], sems.at[FWD_RECV, g], p).start()
 
-        peers(one, ISSUE)
+        peers(one, ISSUE, first, stop)
+        if stop < nsub:
+            return
         pack_forward(g, me)
         pltpu.make_async_copy(fsend.at[g, me], frecv.at[g, me], sems.at[FWD_RECV, g]).start()
 
@@ -154,14 +159,15 @@
             high = v.astype(jnp.bfloat16).astype(jnp.float32)
             lhs[:, k * width:(k + 1) * width] = jnp.where(top, high, v - high).astype(jnp.bfloat16)
 
-        def column(n, acc):
-            cols = pl.ds(pl.multiple_of(n * width, width), width)
-            o = jnp.dot(lhs[...], inv[:, cols], preferred_element_type=jnp.float32)
+        acc = zero
+        for n in range(nslot):
+            o = jnp.dot(
+                lhs[...], inv[:, n * width:(n + 1) * width], preferred_element_type=jnp.float32
+            )
             o = o + swap(o)
             resp[n] = o
-            return acc + load[n] * o
-
-        return lax.fori_loop(0, nslot, column, zero)
+            acc = acc + load[n] * o
+        return acc
 
     def pack_return(g, s):
         a = resp[jnp.maximum(slot_sm[s, 0, 0], 0)]
@@ -209,12 +215,14 @@
         wait_bytes(all_in.at[g, pl.ds(0, nsub - 1)], sems.at[ALL_SEND, g])
         return jnp.sum(all_in[g], axis=0)
 
-    def send_back(g):
+    def send_back(g, first=1, stop=nsub):
         def one(p):
             pack_return(g, p)
             remote(rsend.at[g, p], rrecv[g].at[me], sems.at[RET_SEND, g], sems.at[RET_RECV, g], p).start()
 
-        peers(one, ISSUE)
+        peers(one, ISSUE, first, stop)
+        if stop < nsub:
+            return
         pack_return(g, me)
         pltpu.make_async_copy(rsend.at[g, me], rrecv[g].at[me], sems.at[RET_RECV, g]).start()
 
@@ -237,7 +245,7 @@
         beta = rr / rr_old
         return beta, image + precv[par, g, 0] - beta * beta * curve_old
 
-    def receive_return(g, par, rr_old, curve_old):
+    def receive_return(g, par, rr_old, curve_old, meanwhile):
         wait_bytes(rrecv[g], sems.at[RET_RECV, g])
         image, rr = unfold(g, receive_far(g))
 
@@ -258,6 +266,7 @@
         lax.fori_loop(half // 8, half // 4, pick, 0)
         second = partner(g, par, 1)
         second.start()
+        meanwhile()
         first.wait()
         beta, curve = steps(g, par, image, rr, rr_old, curve_old)
         alpha = rr / curve
@@ -322,13 +331,18 @@
                 send_far(g - 1)
             send_near(g, row)
             (forward_sent if g == 0 else return_sent)(1 - g)
-            send_back(g)
-        for g in range(GROUPS):
-            carry[g] = receive_return(g, lax.rem(k, 2), *carry[g][1:])
-            if g == 0:
-                send_far(GROUPS - 1)
-            (return_sent if g == 0 else forward_sent)(1 - g)
-            forward(g)
+            send_back(g, 1, nsub if g == 0 else CUT)
+
+        def rest_of_return():
+            send_back(1, CUT)
+            send_far(1)
+
+        carry[0] = receive_return(0, lax.rem(k, 2), *carry[0][1:], rest_of_return)
+        return_sent(1)
+        forward(0, 1, CUT)
+        carry[1] = receive_return(1, lax.rem(k, 2), *carry[1][1:], lambda: forward(0, CUT))
+        forward_sent(0)
+        forward(1)
         return tuple(carry)
 
     one = jnp.ones(tile, jnp.float32)
@@ -338,14 +352,15 @@
         send_all(g, sums_row(receive_forward(g), carry[g][0]))
         if g == 0:
             forward_sent(1)
+    ends = []
+    for g in range(GROUPS):
+        ends.append(unfold(g, receive_all(g)))
+        partner(g, par, 2).start()
     last = []
     for g in range(GROUPS):
-        image, rr = unfold(g, receive_all(g))
-        copy = partner(g, par, 2)
-        copy.start()
-        copy.wait()
-        beta, curve = steps(g, par, image, rr, carry[g][1], carry[g][2])
-        last.append((rr / curve, beta))
+        partner(g, par, 2).wait()
+        beta, curve = steps(g, par, *ends[g], carry[g][1], carry[g][2])
+        last.append((ends[g][1] / curve, beta))
 
     def finish(i, c):
         for u in range(UNROLL):

time: 130 us -> 125 us (0.962)
  Pallas kernels: 125 us -> 121 us
    pallas_call x1, Pallas kernels: 125 us -> 121 us  [on_device(): pl.pallas_call(functools.partial(kernel, nsub, npatch, nslot, width), out...]
where the time goes in v3:
time: 125 us
  Pallas kernels  121 us (97%)
  local copies, waits for them, and re-layouts  2.99 us (2%)
  other arithmetic  1.71 us (1%)
    pallas_call x1, Pallas kernels, on_device(): pl.pallas_call(functools.partial(kernel, nsub, npatch, nslot, width), out...  121 us

profile of v3, /device:TPU:1, one launch (start us, length us, event | category | flops | bytes accessed | tf_op | source)
XLA Modules:
  0.0 125.3 jit_solution(7594891525829573775)
XLA Ops:
  0.0 0.7 convert_element_type.7.keep
  0.7 0.8 fusion.1
  1.4 0.2 convert_reduce_fusion.rank
  1.6 0.1 select_reduce_fusion
  1.7 0.1 sub.7
  1.9 0.0 copy-start
  1.9 1.0 copy-done
  2.9 0.0 copy-start.1
  2.9 0.8 copy-done.1
  3.8 120.5 %shard_map.73 = f32[64,8,256]{2,1,0:T(8,128)S(1)} custom-call(s32[128]{0:T(128)S(1)} %get-tuple-element.6.src, s32[64]{0:T(128)S(1)} %get-tuple-element.7.own, s32[64]{0:T(128)S(1)} %convert_reduce_fusion.rank, f32[64]{0:T(128)S(1)} %convert_element_type.7.keep, f32[64,256]{1,0:T(8,128)S(1)} %copy-done.1, s32[64,1,128]{2,1,0:T(1,128)S(1)} %pad.4.slots, ...), custom_call_target="tpu_custom_call" | custom-call | tf_op jit(solution)/shard_map/pallas_call | solution.py:402
  124.3 1.0 copy.13
  (3 shorter events, 0.0 us)
Async XLA Ops:
  1.9 1.0 copy-start
  2.9 0.8 copy-start.1

commit v4 on v3

--- a/solution.py
+++ b/solution.py
@@ -99,7 +99,7 @@
         rows = comp[pl.ds(pl.multiple_of(i * UNROLL, UNROLL), UNROLL), :]
         for u in range(UNROLL):
             p = i * UNROLL + u
-            v = keep[p] * rhs[p]
+            v = keep[p].astype(jnp.float32) * rhs[p]
             w = swap(v)
             for g in range(GROUPS):
                 t = jnp.where(top, v, w) if g == 0 else jnp.where(top, w, v)
@@ -286,7 +286,7 @@
                     c = jnp.broadcast_to(rows[u:u + 1, :], tile)
                     r = res[g, q]
                     d = r + beta * dirn[g, q]
-                    f = keep[q] * (v + c * r) + beta * imag[g, q]
+                    f = keep[q].astype(jnp.float32) * (v + c * r) + beta * imag[g, q]
                     dirn[g, q] = d
                     imag[g, q] = f
                     sol[g, q] = sol[g, q] + alpha * d
@@ -389,7 +389,6 @@
     source = jnp.sum(jnp.where(placed, patch[None, :], 0), axis=1)
     sent_slot = jnp.sum(jnp.where(placed, slot[None, :] + 1, 0), axis=1) - 1
     slots = jnp.pad(sent_slot.reshape(nsub, 1, ROOM), ((0, 0), (0, 0), (0, 128 - ROOM)))
-    keep = active.astype(jnp.float32)
 
     f32, i32 = jnp.float32, jnp.int32
     vmem = pl.BlockSpec(memory_space=pltpu.VMEM)
@@ -432,7 +431,7 @@
         compiler_params=pltpu.CompilerParams(
             collective_id=0, has_side_effects=True, vmem_limit_bytes=48 * 2**20
         ),
-    )(source, owner, rank, keep, compliance, slots, rhs, inverse[0, 0])
+    )(source, owner, rank, active, compliance, slots, rhs, inverse[0, 0])
     return jnp.transpose(result, (1, 0, 2))
 
 

time: 125 us -> 126 us (level)
    unnamed x4 -> x6, local copies, waits for them, and re-layouts: 1.88 us -> 2.53 us
where the time goes in v4:
time: 126 us; the launch traced here: 125 us
  Pallas kernels  121 us (96%)
  local copies, waits for them, and re-layouts  3.64 us (3%)
    pallas_call x1, Pallas kernels, on_device(): pl.pallas_call(functools.partial(kernel, nsub, npatch, nslot, width), out...  121 us
    unnamed x6, local copies, waits for them, and re-layouts  2.53 us

profile of v4, /device:TPU:1, one launch (start us, length us, event | category | flops | bytes accessed | tf_op | source)
XLA Modules:
  0.0 125.3 jit_solution(18245451351391179557)
XLA Ops:
  0.0 0.8 fusion.1
  0.8 0.2 convert_reduce_fusion.rank
  0.9 0.1 select_reduce_fusion
  1.1 0.1 sub.7
  1.2 0.0 copy-start
  1.2 1.0 copy-done
  2.3 0.0 copy-start.1
  2.3 0.8 copy-done.1
  3.1 0.0 copy-start.2
  3.1 0.7 copy-done.2
  3.8 120.6 %shard_map.73 = f32[64,8,256]{2,1,0:T(8,128)S(1)} custom-call(s32[128]{0:T(128)S(1)} %get-tuple-element.6.src, s32[64]{0:T(128)S(1)} %get-tuple-element.7.own, s32[64]{0:T(128)S(1)} %convert_reduce_fusion.rank, s32[64]{0:T(128)S(1)} %copy-done.2, f32[64,256]{1,0:T(8,128)S(1)} %copy-done.1, s32[64,1,128]{2,1,0:T(1,128)S(1)} %pad.4.slots, ...), custom_call_target="tpu_custom_call" | custom-call | tf_op jit(solution)/shard_map/pallas_call | solution.py:401
  124.4 1.0 copy.13
  (3 shorter events, 0.0 us)
Async XLA Ops:
  1.2 1.0 copy-start
  2.3 0.8 copy-start.1
  3.1 0.7 copy-start.2
